TPU v7x, 256 devices: a whole 4x4x8 slice. The times are simulated.
256 devices in a mesh: row: 64 (over z_hi, y, x), rep: 4 (over z_lo, core).
Axes of the slice: x: 4, y: 4, z: 8 (z_hi: 4, z_lo: 2; z = z_hi * 2 + z_lo), core: 2. Of those that a mesh axis runs over, the one named last changes fastest.
Arguments:
- features: bfloat16 [32768, 128], P('row'), may hold values from -6 to 6
- weight_one: bfloat16 [128, 128], replicated, may hold values from -0.5 to 0.5
- weight_two: bfloat16 [128, 128], replicated, may hold values from -0.5 to 0.5
- cotangent: bfloat16 [32768, 128], P('row'), may hold values from -0.03125 to 0.03125
- adj_tiles: bfloat16 [64, 64, 16, 128, 128], P('row', 'rep'), may hold values from -0.09375 to 0.09375
- tile_rows: int32 [64, 64, 16], P('row', 'rep'), may hold values from 0 to 3, as said below
- tile_cols: int32 [64, 64, 16], P('row', 'rep'), may hold values from 0 to 3
- tile_counts: int32 [64, 64], P('row', 'rep'), may hold values from 0 to 16, as said below
Outputs:
- output: bfloat16 [32768, 128], P('row')
- grad_one: float32 [128, 128], replicated
- grad_two: float32 [128, 128], replicated
Inputs may be any that keep to these rules, and one draw needn't show every extreme that they name: Only slots 0 to tile_counts[b, s] - 1 of block-row b and section s are live; the other slots carry arbitrary tiles and indices that are not part of A. Section b of block-row b holds 16 live slots; many other sections hold none. `tile_rows`: the (row, column) pairs of the slots of one block-row and section are distinct.
All inputs are finite; a program needn't handle non-finite values.
Results may differ from a plain program's by a relative error of at most 0.0065.
Values may be sent and summed in bfloat16 or wider, within the bound.
A program may use at most 192 MiB of HBM per device.

v0:
```python
from functools import partial
import jax
import jax.numpy as jnp
from jax import lax
from jax.sharding import PartitionSpec as P

TILE = 128


def gelu_value(values):
    return values * 0.5 * (1.0 + lax.erf(values * 0.7071067811865476))


def gelu_slope(values):
    normal_cdf = 0.5 * (1.0 + lax.erf(values * 0.7071067811865476))
    return normal_cdf + values * jnp.exp(-0.5 * values * values) * 0.3989422804014327


def row_contract(left, right):
    return lax.dot_general(
        left, right, (((0,), (0,)), ((), ())), preferred_element_type=jnp.float32
    )


def section_work(running, pieces, section_tiles, section_rows, section_cols, live_count):
    slot_total = section_tiles.shape[0]
    count_tiles = running.shape[0]
    sources = jnp.take(pieces, section_cols, axis=0)
    products = jnp.einsum(
        "mij,mjf->mif", section_tiles, sources, preferred_element_type=jnp.float32
    )
    live_mask = jnp.arange(slot_total, dtype=jnp.int32) < live_count
    onehot = jnp.where(
        live_mask[:, None]
        & (section_rows[:, None] == jnp.arange(count_tiles, dtype=jnp.int32)[None, :]),
        1.0,
        0.0,
    ).astype(jnp.float32)
    return running + jnp.einsum("mk,mif->kif", onehot, products, precision=lax.Precision.HIGHEST)


def propagate(tile_data, row_ids, col_ids, live_counts, own_block):
    section_total = tile_data.shape[0]
    block_rows = own_block.shape[0]
    count_tiles = block_rows // TILE
    width = own_block.shape[1]
    first_section = lax.axis_index("rep") * section_total

    def pick(section_id):
        return (
            lax.dynamic_index_in_dim(tile_data, section_id, 0, keepdims=False),
            lax.dynamic_index_in_dim(row_ids, section_id, 0, keepdims=False),
            lax.dynamic_index_in_dim(col_ids, section_id, 0, keepdims=False),
            lax.dynamic_index_in_dim(live_counts, section_id, 0, keepdims=False),
        )

    zeros = jnp.zeros((count_tiles, TILE, width), jnp.float32)
    kept_total = section_total * block_rows
    kept_base = first_section * block_rows
    empty = jnp.zeros((kept_total, width), own_block.dtype)
    piece = lax.all_gather(own_block, "row", axis=0, tiled=True)
    piece_rows = piece.shape[0]
    padding = jnp.zeros((piece_rows, width), empty.dtype)
    widened = jnp.concatenate([padding, empty, padding], axis=0)
    offset = jnp.clip(jnp.int32(0) - kept_base + piece_rows, 0, kept_total + piece_rows)
    widened = lax.dynamic_update_slice_in_dim(widened, piece, offset, 0)
    kept = widened[piece_rows : piece_rows + kept_total]
    kept = kept.reshape(section_total, count_tiles, TILE, width)

    def kept_step(section_id, running):
        pieces = lax.dynamic_index_in_dim(kept, section_id, 0, keepdims=False)
        return section_work(running, pieces, *pick(section_id))

    summed = lax.fori_loop(0, section_total, kept_step, zeros)
    return summed.reshape(block_rows, width)


def whole_sum(partial_rows):
    return lax.psum(partial_rows, "rep")


def per_device(
    features, weight_one, weight_two, cotangent, adj_tiles, tile_rows, tile_cols, tile_counts
):
    spread = partial(propagate, adj_tiles[0], tile_rows[0], tile_cols[0], tile_counts[0])
    d_two = lax.dot_general(
        cotangent, weight_two, (((1,), (1,)), ((), ())), preferred_element_type=jnp.float32
    ).astype(jnp.bfloat16)
    s_one = whole_sum(spread(features)).astype(jnp.bfloat16)
    pre_one = jnp.dot(s_one, weight_one, preferred_element_type=jnp.float32)
    hidden = gelu_value(pre_one).astype(jnp.bfloat16)
    s_two = whole_sum(spread(hidden)).astype(jnp.bfloat16)
    output = jnp.dot(s_two, weight_two, preferred_element_type=jnp.float32).astype(jnp.bfloat16)
    grad_two = lax.psum(row_contract(s_two, cotangent), "row")
    d_hidden = whole_sum(spread(d_two))
    d_pre = (d_hidden * gelu_slope(pre_one)).astype(jnp.bfloat16)
    grad_one = lax.psum(row_contract(s_one, d_pre), "row")
    return (output, grad_one, grad_two)


def solution(mesh):
    placed = (
        P("row", None),
        P(),
        P(),
        P("row", None),
        P("row", "rep", None, None, None),
        P("row", "rep", None),
        P("row", "rep", None),
        P("row", "rep"),
    )
    return jax.shard_map(
        per_device,
        mesh=mesh,
        in_specs=placed,
        out_specs=(P("row", None), P(), P()),
        check_vma=False,
    )
```

profile of v0, /device:TPU:2, one launch (start us, length us, event | category | flops | bytes accessed | tf_op | source)
XLA Modules:
  0.0 1363.7 jit_solution(14181095154365439595)
XLA Ops:
  8.1 1.6 convolution_convert_fusion
  10.6 3.9 broadcast.50
  14.4 15.8 %pad_maximum_fusion = bf16[73728,128]{1,0:T(8,128)(2,1)S(1)} fusion(bf16[32768,128]{1,0:T(8,128)(2,1)} %broadcast.50, bf16[73728]{0:T(1024)(128)(2,1)S(1)} %pad.1.clone), kind=kLoop, calls=%fused_computation.90 | loop fusion | flops 56623104 | bytes 27410432 | tf_op jit(solution)/shard_map/concatenate | solution.py:64
  30.2 6.4 copy.46
  36.6 5.8 copy-done.1
  42.4 6.5 copy.38
  48.8 73.8 %all-gather.8.cloned.1.call-done = bf16[32768,128]{1,0:T(8,128)(2,1)} async-done(((bf16[512,128]{1,0:T(8,128)(2,1)}), bf16[32768,128]{1,0:T(8,128)(2,1)}) %all-gather.8.cloned.1.call-update) | async-done | bytes 8388624 | tf_op jit(solution)/shard_map/all_gather | solution.py:61
  122.6 39.0 %dynamic_update_slice.11 = bf16[73728,128]{1,0:T(8,128)(2,1)} dynamic-update-slice(bf16[73728,128]{1,0:T(8,128)(2,1)} %copy.46, bf16[32768,128]{1,0:T(8,128)(2,1)} %all-gather.8.cloned.1.call-done, s32[]{:T(128)S(6)} %min.6, s32[]{:T(128)} %constant.163.clone.1) | dynamic-update-slice | bytes 16777220 | tf_op jit(solution)/shard_map/dynamic_update_slice | solution.py:66
  161.7 3.0 slice.20
  164.7 113.0 %while.44 = (s32[]{:T(128)}, f32[4,128,128]{2,0,1:T(4,128)S(1)}, s32[16]{0:T(128)S(1)}, s32[16,16]{1,0:T(8,128)}, bf16[16,16,128,128]{3,2,1,0:T(8,128)(2,1)}, /*...) while((s32[]{:T(128)}, f32[4,128,128]{2,0,1:T(4,128)S(1)}, ...), condition=%wide.region_7.9_spmd.clone, body=%wide.region_6.8_spmd.clone.sunk | while | flops 80086320 | bytes 4985487 | solution.py:74
  176.0 1.5 fusion.124
  183.1 1.4 fusion.124
  197.2 1.4 fusion.124
  204.3 1.4 fusion.124
  218.4 1.4 fusion.124
  232.5 1.4 fusion.124
  278.5 39.1 %dynamic_update_slice.9 = bf16[73728,128]{1,0:T(8,128)(2,1)} dynamic-update-slice(bf16[73728,128]{1,0:T(8,128)(2,1)} %copy-done.1, bf16[32768,128]{1,0:T(8,128)(2,1)} %all-gather.4.cloned.1.call-done, s32[]{:T(128)S(6)} %min.6, s32[]{:T(128)} %constant.163.clone.1) | dynamic-update-slice | bytes 16777220 | tf_op jit(solution)/shard_map/dynamic_update_slice | solution.py:66
  317.6 1.7 slice.18
  319.3 98.5 %while.42 = (s32[]{:T(128)}, f32[4,128,128]{2,0,1:T(4,128)S(1)}, s32[16]{0:T(128)S(1)}, s32[16,16]{1,0:T(8,128)}, bf16[16,16,128,128]{3,2,1,0:T(8,128)(2,1)}, /*...) while((s32[]{:T(128)}, f32[4,128,128]{2,0,1:T(4,128)S(1)}, ...), condition=%wide.region_1.3_spmd.clone, body=%wide.region_0.2_spmd.clone.sunk | while | flops 80086320 | bytes 4985487 | solution.py:74
  335.0 1.4 fusion.112
  341.1 1.4 fusion.112
  347.3 1.4 fusion.112
  353.4 1.4 fusion.112
  359.6 1.4 fusion.112
  365.8 1.4 fusion.112
  371.9 1.4 fusion.112
  378.1 1.4 fusion.112
  384.2 1.4 fusion.112
  396.5 1.4 fusion.112
  408.9 1.4 fusion.112
  417.9 21.4 %all-reduce.9 = bf16[512,128]{1,0:T(8,128)(2,1)S(1)} all-reduce(f32[512,128]{1,0:T(8,128)S(1)} %bitcast.102), channel_id=1, replica_groups=mesh['row'=64,'rep'=4] {'rep'}, use_global_device_ids=true, to_apply=%region_2.4 | all-reduce | flops 65536 | bytes 393216 | tf_op jit(solution)/shard_map/psum | solution.py:79
  440.3 1.9 fusion.69
  442.1 104.2 %all-gather.6.cloned.1.call-done = bf16[32768,128]{1,0:T(8,128)(2,1)} async-done(((bf16[512,128]{1,0:T(8,128)(2,1)}), bf16[32768,128]{1,0:T(8,128)(2,1)}) %all-gather.6.cloned.1.call-update) | async-done | bytes 8388624 | tf_op jit(solution)/shard_map/all_gather | solution.py:61
  546.3 39.1 %dynamic_update_slice.10 = bf16[73728,128]{1,0:T(8,128)(2,1)} dynamic-update-slice(bf16[73728,128]{1,0:T(8,128)(2,1)} %copy.38, bf16[32768,128]{1,0:T(8,128)(2,1)} %all-gather.6.cloned.1.call-done, s32[]{:T(128)S(6)} %min.6, s32[]{:T(128)} %constant.163.clone.1) | dynamic-update-slice | bytes 16777220 | tf_op jit(solution)/shard_map/dynamic_update_slice | solution.py:66
  585.4 1.7 slice.19
  587.2 98.5 %while.43 = (s32[]{:T(128)}, f32[4,128,128]{2,0,1:T(4,128)S(1)}, s32[16]{0:T(128)S(1)}, s32[16,16]{1,0:T(8,128)}, bf16[16,16,128,128]{3,2,1,0:T(8,128)(2,1)}, /*...) while((s32[]{:T(128)}, f32[4,128,128]{2,0,1:T(4,128)S(1)}, ...), condition=%wide.region_4.6_spmd.clone, body=%wide.region_3.5_spmd.clone.sunk | while | flops 80086320 | bytes 4985487 | solution.py:74
  609.0 1.4 fusion.118
  621.3 1.4 fusion.118
  627.5 1.4 fusion.118
  645.9 1.4 fusion.118
  652.1 1.4 fusion.118
  658.2 1.4 fusion.118
  664.4 1.4 fusion.118
  670.5 1.4 fusion.118
  685.7 21.3 %all-reduce.10 = bf16[512,128]{1,0:T(8,128)(2,1)S(1)} all-reduce(f32[512,128]{1,0:T(8,128)S(1)} %bitcast.103), channel_id=1, replica_groups=mesh['row'=64,'rep'=4] {'rep'}, use_global_device_ids=true, to_apply=%region_5.7 | all-reduce | flops 65536 | bytes 393216 | tf_op jit(solution)/shard_map/psum | solution.py:79
  708.8 645.5 %all-reduce.8.cloned.1.call-done = (f32[128,128]{1,0:T(8,128)}, f32[128,128]{1,0:T(8,128)}) async-done(((f32[128,128]{1,0:T(8,128)}, f32[128,128]{1,0:T(8,128)}), (f32[128,128]{1,0:T(8,128)}, f32[128,128]{1,0:T(8,128)})) %all-reduce.8.cloned.1.call-update) | async-done | bytes 131088 | tf_op jit(solution)/shard_map/psum | solution.py:97
  1354.2 1.5 copy.58
  1355.7 1.5 copy.59
  (441 shorter events, 277.4 us)
Async XLA Ops:
  7.2 0.9 copy-start
  7.2 115.4 %all-gather.8.cloned.1.call-start = ((), (), s32[]{:S(2)}) async-start(), calls=%async_computation.2 | async-start | bytes 8519680 | tf_op jit(solution)/shard_map/all_gather | solution.py:61
  9.7 268.8 %all-gather.4.cloned.1.call-start = ((), (), s32[]{:S(2)}) async-start(), calls=%async_computation | async-start | bytes 8519680 | tf_op jit(solution)/shard_map/all_gather | solution.py:61
  10.5 429.8 %all-reduce.6.cloned.1.call-start = ((), (), s32[]{:S(2)}) async-start(), calls=%async_computation.3 | async-start | bytes 524288 | tf_op jit(solution)/shard_map/psum | solution.py:79
  30.2 12.2 copy-start.1
  48.8 115.9 %copy-start.2 = (f32[4,128,128]{2,0,1:T(4,128)S(1)}, f32[4,128,128]{2,0,1:T(4,128)}, u32[]{:S(2)}) copy-start(f32[4,128,128]{2,0,1:T(4,128)} %custom-call.2) | copy-start | bytes 786436
  48.8 115.9 %copy-start.5 = (s32[1,16]{1,0:T(1,128)S(1)}, s32[1,16]{1,0:T(1,128)}, u32[]{:S(2)}) copy-start(s32[1,16]{1,0:T(1,128)} %param.23) | copy-start | bytes 196
  278.4 267.9 %all-gather.6.cloned.1.call-start = ((), (), s32[]{:S(2)}) async-start(), calls=%async_computation.1 | async-start | bytes 8519680 | tf_op jit(solution)/shard_map/all_gather | solution.py:61
  319.3 120.0 %copy-start.4 = (bf16[128,128]{1,0:T(8,128)(2,1)S(1)}, bf16[128,128]{1,0:T(8,128)(2,1)}, u32[]{:S(2)}) copy-start(bf16[128,128]{1,0:T(8,128)(2,1)} %param.17) | copy-start | bytes 98308
  440.2 914.0 %all-reduce.8.cloned.1.call-start = ((), (), s32[]{:S(2)}) async-start(), calls=%async_computation.4 | async-start | bytes 262144 | tf_op jit(solution)/shard_map/psum | solution.py:97
  587.2 120.8 %copy-start.3 = (bf16[128,128]{1,0:T(8,128)(2,1)S(1)}, bf16[128,128]{1,0:T(8,128)(2,1)}, u32[]{:S(2)}) copy-start(bf16[128,128]{1,0:T(8,128)(2,1)} %param.18) | copy-start | bytes 98308
Sparse Core Ops, SparseCore 0:
  11.9 110.6 all-gather.7
  125.9 113.1 all-gather.3
  278.5 46.1 all-reduce.5
  440.3 105.9 all-gather.5
  708.0 646.1 all-reduce.7
where the time goes:
time: 1370 us; the launch traced here: 1360 us
  waiting for transfers between devices  824 us (60%)
  local copies, waits for them, and re-layouts  259 us (19%)
  matrix products  141 us (10%)
  other arithmetic  80.6 us (6%)
  blocking collectives  42.8 us (3%)
  between operations  14 us (1%)
    psum x1, waiting for transfers between devices, per_device(): grad_one = lax.psum(row_contract(s_one, d_pre), 'row')  645 us
    all_gather x3, waiting for transfers between devices, propagate(): piece = lax.all_gather(own_block, 'row', axis=0, tiled=True)  178 us
    dynamic_update_slice x3, local copies, waits for them, and re-layouts, propagate(): widened = lax.dynamic_update_slice_in_dim(widened, piece, offset, 0)  117 us
    dot_general x48, matrix products, section_work(): jnp.einsum('mij,mjf->mif', section_tiles, sources, preferred_element_type...  68 us
    dot_general x48, matrix products, section_work(): jnp.einsum('mk,mif->kif', onehot, products, precision=lax.Precision.HIGHEST)  66.7 us
    psum x2, blocking collectives, whole_sum(): return lax.psum(partial_rows, 'rep')  42.8 us
    eq x48, local copies, waits for them, and re-layouts, section_work(): section_rows[:, None] == jnp.arange(count_tiles, dtype=jnp.int32)[None, :]  33.5 us
    and x48, other arithmetic, section_work(): sources = jnp.take(pieces, section_cols, axis=0)  33.4 us
  transfers between devices with their start and end apart: 5, of which 3 were waited for; matrix products, arithmetic and copies ran while one was open for 24% of the time, Pallas kernels for 0%

commit v1 on v0

--- a/solution.py
+++ b/solution.py
@@ -5,6 +5,11 @@
 from jax.sharding import PartitionSpec as P
 
 TILE = 128
+
+
+def handle_halves(array_here, mesh_name):
+    now = jax.lax.all_gather(array_here, mesh_name)
+    return jnp.sum(now, axis=0)
 
 
 def gelu_value(values):
@@ -76,7 +81,7 @@
 
 
 def whole_sum(partial_rows):
-    return lax.psum(partial_rows, "rep")
+    return handle_halves(partial_rows, "rep")
 
 
 def per_device(

time: 1370 us -> 1280 us (0.934)
  waiting for transfers between devices: 824 us -> 752 us
  blocking collectives: 42.8 us -> 0 us
  local copies, waits for them, and re-layouts: 259 us -> 276 us
    all_gather x3, waiting for transfers between devices: 178 us -> 75.8 us  [propagate(): piece = lax.all_gather(own_block, 'row', axis=0, tiled=True)]
    psum x2 -> x0, blocking collectives: 42.8 us -> none  [whole_sum(): return lax.psum(partial_rows, 'rep')]
    dynamic_slice x48, local copies, waits for them, and re-layouts: 28.1 us -> 60.8 us  [pick(): lax.dynamic_index_in_dim(live_counts, section_id, 0, keepdims=False)]
    all_gather x0 -> x3, waiting for transfers between devices: none -> 26.7 us  [handle_halves(): now = jax.lax.all_gather(array_here, mesh_name)]
    squeeze x48, local copies, waits for them, and re-layouts: 15.4 us -> 0.86 us  [kept_step(): pieces = lax.dynamic_index_in_dim(kept, section_id, 0, keepdims=False)]
  transfers between devices with their start and end apart: 5 -> 7, of which waited for: 3 -> 4; matrix products, arithmetic and copies ran while one was open for 24% -> 38% of each run, Pallas kernels for 0% -> 0%
where the time goes in v1:
time: 1280 us; the launch traced here: 1270 us
  waiting for transfers between devices  752 us (59%)
  local copies, waits for them, and re-layouts  276 us (22%)
  matrix products  141 us (11%)
  other arithmetic  84.9 us (7%)
  between operations  14.3 us (1%)
    psum x1, waiting for transfers between devices, per_device(): grad_one = lax.psum(row_contract(s_one, d_pre), 'row')  648 us
    dynamic_update_slice x3, local copies, waits for them, and re-layouts, propagate(): widened = lax.dynamic_update_slice_in_dim(widened, piece, offset, 0)  117 us
    all_gather x3, waiting for transfers between devices, propagate(): piece = lax.all_gather(own_block, 'row', axis=0, tiled=True)  75.8 us
    dot_general x48, matrix products, section_work(): jnp.einsum('mij,mjf->mif', section_tiles, sources, preferred_element_type...  68 us
    dot_general x48, matrix products, section_work(): jnp.einsum('mk,mif->kif', onehot, products, precision=lax.Precision.HIGHEST)  66.7 us
    dynamic_slice x48, local copies, waits for them, and re-layouts, pick(): lax.dynamic_index_in_dim(live_counts, section_id, 0, keepdims=False)  60.8 us
    eq x48, local copies, waits for them, and re-layouts, section_work(): section_rows[:, None] == jnp.arange(count_tiles, dtype=jnp.int32)[None, :]  33.5 us
    and x48, other arithmetic, section_work(): sources = jnp.take(pieces, section_cols, axis=0)  33.4 us
  transfers between devices with their start and end apart: 7, of which 4 were waited for; matrix products, arithmetic and copies ran while one was open for 38% of the time, Pallas kernels for 0%

profile of v1, /device:TPU:2, one launch (start us, length us, event | category | flops | bytes accessed | tf_op | source)
XLA Modules:
  0.0 1270.3 jit_solution(8374653240530133714)
XLA Ops:
  8.1 1.6 convolution_convert_fusion
  9.8 3.9 broadcast.50
  13.7 15.8 %pad_maximum_fusion = bf16[73728,128]{1,0:T(8,128)(2,1)S(1)} fusion(bf16[32768,128]{1,0:T(8,128)(2,1)} %broadcast.50, bf16[73728]{0:T(1024)(128)(2,1)S(1)} %pad.1.clone), kind=kLoop, calls=%fused_computation.90 | loop fusion | flops 56623104 | bytes 27410432 | tf_op jit(solution)/shard_map/concatenate | solution.py:69
  29.4 6.5 copy.46
  36.0 5.5 copy-done.1
  41.5 6.5 copy.39
  48.0 74.1 %all-gather.7.cloned.1.call-done = bf16[32768,128]{1,0:T(8,128)(2,1)} async-done(((bf16[512,128]{1,0:T(8,128)(2,1)}), bf16[32768,128]{1,0:T(8,128)(2,1)}) %all-gather.7.cloned.1.call-update) | async-done | bytes 8388624 | tf_op jit(solution)/shard_map/all_gather | solution.py:66
  122.0 39.1 %dynamic_update_slice.9 = bf16[73728,128]{1,0:T(8,128)(2,1)} dynamic-update-slice(bf16[73728,128]{1,0:T(8,128)(2,1)} %copy-done.1, bf16[32768,128]{1,0:T(8,128)(2,1)} %all-gather.7.cloned.1.call-done, s32[]{:T(128)S(6)} %min.6, s32[]{:T(128)} %constant.164.clone.1) | dynamic-update-slice | bytes 16777220 | tf_op jit(solution)/shard_map/dynamic_update_slice | solution.py:71
  161.1 1.7 slice.18
  162.8 109.0 %while.42 = (s32[]{:T(128)}, f32[4,128,128]{2,0,1:T(4,128)S(1)}, s32[16]{0:T(128)}, s32[16,16]{1,0:T(8,128)}, bf16[16,16,128,128]{3,2,1,0:T(8,128)(2,1)}, /*inde...) while((s32[]{:T(128)}, f32[4,128,128]{2,0,1:T(4,128)S(1)}, ...), condition=%wide.region_1.3_spmd.clone, body=%wide.region_0.2_spmd.clone.sunk | while | flops 80086320 | bytes 4985487 | solution.py:79
  173.6 1.4 fusion.112
  180.4 1.4 fusion.112
  207.7 1.4 fusion.112
  221.3 1.4 fusion.112
  241.8 1.4 fusion.112
  248.6 1.4 fusion.112
  272.7 39.1 %dynamic_update_slice.11 = bf16[73728,128]{1,0:T(8,128)(2,1)} dynamic-update-slice(bf16[73728,128]{1,0:T(8,128)(2,1)} %copy.46, bf16[32768,128]{1,0:T(8,128)(2,1)} %all-gather.15.cloned.1.call-done, s32[]{:T(128)S(6)} %min.6, s32[]{:T(128)} %constant.164.clone.1) | dynamic-update-slice | bytes 16777220 | tf_op jit(solution)/shard_map/dynamic_update_slice | solution.py:71
  311.8 1.7 slice.20
  315.8 110.6 %while.44 = (s32[]{:T(128)}, f32[4,128,128]{2,0,1:T(4,128)S(1)}, s32[16]{0:T(128)}, s32[16,16]{1,0:T(8,128)}, bf16[16,16,128,128]{3,2,1,0:T(8,128)(2,1)}, /*inde...) while((s32[]{:T(128)}, f32[4,128,128]{2,0,1:T(4,128)S(1)}, ...), condition=%wide.region_7.9_spmd.clone, body=%wide.region_6.8_spmd.clone.sunk | while | flops 80086320 | bytes 4985487 | solution.py:79
  326.9 1.4 fusion.124
  333.8 1.4 fusion.124
  340.7 1.4 fusion.124
  347.6 1.4 fusion.124
  361.4 1.4 fusion.124
  368.3 1.4 fusion.124
  375.3 1.4 fusion.124
  396.0 1.4 fusion.124
  402.9 1.4 fusion.124
  409.8 1.4 fusion.124
  416.7 1.4 fusion.124
  427.2 1.7 all-gather.11.cloned.1.call-done
  429.0 39.1 %dynamic_update_slice.10 = bf16[73728,128]{1,0:T(8,128)(2,1)} dynamic-update-slice(bf16[73728,128]{1,0:T(8,128)(2,1)} %copy.39, bf16[32768,128]{1,0:T(8,128)(2,1)} %all-gather.11.cloned.1.call-done, s32[]{:T(128)S(6)} %min.6, s32[]{:T(128)} %constant.164.clone.1) | dynamic-update-slice | bytes 16777220 | tf_op jit(solution)/shard_map/dynamic_update_slice | solution.py:71
  468.1 1.7 slice.19
  469.8 109.0 %while.43 = (s32[]{:T(128)}, f32[4,128,128]{2,0,1:T(4,128)S(1)}, s32[16]{0:T(128)}, s32[16,16]{1,0:T(8,128)}, bf16[16,16,128,128]{3,2,1,0:T(8,128)(2,1)}, /*inde...) while((s32[]{:T(128)}, f32[4,128,128]{2,0,1:T(4,128)S(1)}, ...), condition=%wide.region_4.6_spmd.clone, body=%wide.region_3.5_spmd.clone.sunk | while | flops 80086320 | bytes 4985487 | solution.py:79
  473.8 1.4 fusion.118
  480.7 1.4 fusion.118
  487.5 1.4 fusion.118
  501.1 1.4 fusion.118
  507.9 1.4 fusion.118
  528.3 1.4 fusion.118
  535.1 1.4 fusion.118
  555.6 1.4 fusion.118
  562.4 1.4 fusion.118
  581.9 26.7 %all-gather.13.cloned.1.call-done = f32[4,512,128]{2,1,0:T(8,128)} async-done(((f32[1,512,128]{2,1,0:T(8,128)}), f32[4,512,128]{2,1,0:T(8,128)}) %all-gather.13.cloned.1.call-update) | async-done | bytes 1048592 | tf_op jit(solution)/shard_map/all_gather | solution.py:11
  610.7 1.6 convolution_convert_fusion.1
  612.3 648.2 %all-reduce.3.cloned.1.call-done = (f32[128,128]{1,0:T(8,128)}, f32[128,128]{1,0:T(8,128)}) async-done(((f32[128,128]{1,0:T(8,128)}, f32[128,128]{1,0:T(8,128)}), (f32[128,128]{1,0:T(8,128)}, f32[128,128]{1,0:T(8,128)})) %all-reduce.3.cloned.1.call-update) | async-done | bytes 131088 | tf_op jit(solution)/shard_map/psum | solution.py:102
  1260.5 1.5 copy.55
  1262.0 1.5 copy.56
  (444 shorter events, 299.4 us)
Async XLA Ops:
  7.2 0.9 copy-start
  7.2 114.9 %all-gather.7.cloned.1.call-start = ((), (), s32[]{:S(2)}) async-start(), calls=%async_computation | async-start | bytes 8519680 | tf_op jit(solution)/shard_map/all_gather | solution.py:66
  7.9 264.8 %all-gather.15.cloned.1.call-start = ((), (), s32[]{:S(2)}) async-start(), calls=%async_computation.4 | async-start | bytes 8519680 | tf_op jit(solution)/shard_map/all_gather | solution.py:66
  9.7 303.8 %all-gather.9.cloned.1.call-start = ((), (), s32[]{:S(2)}) async-start(), calls=%async_computation.1 | async-start | bytes 1310720 | tf_op jit(solution)/shard_map/all_gather | solution.py:11
  29.4 12.1 copy-start.1
  272.6 156.4 %all-gather.11.cloned.1.call-start = ((), (), s32[]{:S(2)}) async-start(), calls=%async_computation.2 | async-start | bytes 8519680 | tf_op jit(solution)/shard_map/all_gather | solution.py:66
  272.7 42.2 %copy-start.3 = (bf16[128,128]{1,0:T(8,128)(2,1)S(1)}, bf16[128,128]{1,0:T(8,128)(2,1)}, u32[]{:S(2)}) copy-start(bf16[128,128]{1,0:T(8,128)(2,1)} %param.17) | copy-start | bytes 98308
  315.8 263.8 %all-gather.17.cloned.1.call-start = ((), (), s32[]{:S(2)}) async-start(), calls=%async_computation.5 | async-start | bytes 1310720 | tf_op jit(solution)/shard_map/all_gather | solution.py:11
  427.2 181.4 %all-gather.13.cloned.1.call-start = ((), (), s32[]{:S(2)}) async-start(), calls=%async_computation.3 | async-start | bytes 1310720 | tf_op jit(solution)/shard_map/all_gather | solution.py:11
  469.8 111.2 %copy-start.2 = (f32[512,128]{1,0:T(8,128)S(1)}, f32[512,128]{1,0:T(8,128)}, u32[]{:S(2)}) copy-start(f32[512,128]{1,0:T(8,128)} %get-tuple-element.502) | copy-start | bytes 786436
  579.6 680.9 %all-reduce.3.cloned.1.call-start = ((), (), s32[]{:S(2)}) async-start(), calls=%async_computation.6 | async-start | bytes 262144 | tf_op jit(solution)/shard_map/psum | solution.py:102
Sparse Core Ops, SparseCore 0:
  11.3 110.6 all-gather.6
  125.9 113.0 all-gather.14
  272.7 28.7 all-gather.8
  315.9 113.0 all-gather.10
  430.6 28.8 all-gather.16
  579.7 28.8 all-gather.12
  611.8 648.6 all-reduce.2
